TPU v7x, 32 devices: a whole 2x2x4 slice. The times are simulated.
32 devices in a mesh: section: 2 (over y), tensor: 4 (over z), fsdp: 4 (over x, core).
Axes of the slice: x: 2, y: 2, z: 4, core: 2. Of those that a mesh axis runs over, the one named last changes fastest.
Arguments:
- images: bfloat16 [2, 4, 729, 1152], P(None, 'fsdp'), may hold values from -6 to 6
- cotangent: bfloat16 [2, 4, 729, 1152], P(None, 'fsdp'), may hold values from -6 to 6
- qkv_weight: bfloat16 [2, 3, 1152, 1152], P('section', None, 'fsdp', 'tensor'), may hold values from -1 to 1
- qv_bias: bfloat16 [2, 2, 1152], P('section', None, 'tensor'), may hold values from -3 to 3
- out_weight: bfloat16 [2, 1152, 1152], P('section', 'tensor', 'fsdp'), may hold values from -0.75 to 0.75
- up_weight: bfloat16 [2, 1152, 4304], P('section', 'fsdp', 'tensor'), may hold values from -0.1875 to 0.1875
- up_bias: bfloat16 [2, 4304], P('section', 'tensor'), may hold values from -3 to 3
- down_weight: bfloat16 [2, 4304, 1152], P('section', 'tensor', 'fsdp'), may hold values from -0.09375 to 0.09375
- gains: bfloat16 [2, 2, 1152], P('section', None, 'fsdp'), may hold values from 0.099609375 to 1.8984375
- shifts: bfloat16 [2, 4, 1152], P('section', None, 'fsdp'), may hold values from -3 to 3
Outputs:
- section_outputs: bfloat16 [2, 2, 4, 729, 1152], P('section', None, 'fsdp')
- input_grads: bfloat16 [2, 2, 4, 729, 1152], P('section', None, 'fsdp')
- grad_qkv: float32 [2, 3, 1152, 1152], P('section', None, 'fsdp', 'tensor')
- grad_qv_bias: float32 [2, 2, 1152], P('section', None, 'tensor')
- grad_out: float32 [2, 1152, 1152], P('section', 'tensor', 'fsdp')
- grad_up: float32 [2, 1152, 4304], P('section', 'fsdp', 'tensor')
- grad_up_bias: float32 [2, 4304], P('section', 'tensor')
- grad_down: float32 [2, 4304, 1152], P('section', 'tensor', 'fsdp')
- grad_gains: float32 [2, 2, 1152], P('section', None, 'fsdp')
- grad_shifts: float32 [2, 4, 1152], P('section', None, 'fsdp')
All inputs are finite; a program needn't handle non-finite values.
Results may differ from a plain program's by a relative error of at most 0.013.
Values may be sent and summed in bfloat16 or wider, within the bound.
A program may use at most 256 MiB of HBM per device.

v0:
```python
import jax
import jax.numpy as jnp
from jax import lax
from jax.sharding import PartitionSpec as P

HD = 72
NORM_EPS = 1e-06
GELU_ROOT = 0.7978845608028654
GELU_CUBIC = 0.044715


def from_behind(value, axis, steps):
    count = lax.axis_size(axis)
    leading, last = (max(0, -steps), min(count, count - steps))
    return lax.ppermute(value, axis, [(source, source + steps) for source in range(leading, last)])


def gelu_value(value):
    return 0.5 * value * (1.0 + jnp.tanh(GELU_ROOT * (value + GELU_CUBIC * value * value * value)))


def gelu_slope(value):
    inner = jnp.tanh(GELU_ROOT * (value + GELU_CUBIC * value * value * value))
    return 0.5 * (1.0 + inner) + 0.5 * value * (1.0 - inner * inner) * GELU_ROOT * (
        1.0 + 3.0 * GELU_CUBIC * value * value
    )


def norm_forward(token_rows, gain, shift):
    mean_row = jnp.mean(token_rows, axis=-1, keepdims=True)
    centred = token_rows - mean_row
    inverse = lax.rsqrt(jnp.mean(centred * centred, axis=-1, keepdims=True) + NORM_EPS)
    normed = centred * inverse
    return (normed * gain + shift, normed, inverse)


def norm_backward(grad_normed, normed, inverse, gain):
    scaled = grad_normed * gain
    inner = (
        scaled
        - jnp.mean(scaled, axis=-1, keepdims=True)
        - normed * jnp.mean(scaled * normed, axis=-1, keepdims=True)
    )
    return (inverse * inner, jnp.sum(grad_normed * normed, axis=0), jnp.sum(grad_normed, axis=0))


def layer_forward(layer_input, weights, qv_bias, up_bias):
    qkv_weight, out_weight, up_weight, down_weight, gains, shifts = weights
    image_count, seq_len, model_width = layer_input.shape
    local_heads = qkv_weight.shape[2] // HD
    score_scale = HD ** (-0.5)
    gain_rows = gains.astype(jnp.float32)
    shift_rows = shifts.astype(jnp.float32)
    token_rows = layer_input.astype(jnp.float32).reshape(-1, model_width)
    normed_one = norm_forward(token_rows, gain_rows[0], shift_rows[0])[0].astype(jnp.bfloat16)
    projected = jnp.einsum(
        "td,cde->cte", normed_one, qkv_weight, preferred_element_type=jnp.float32
    )
    bias_rows = qv_bias.astype(jnp.float32)
    queries = (projected[0] + bias_rows[0]).astype(jnp.bfloat16)
    key_rows = projected[1].astype(jnp.bfloat16)
    values = (projected[2] + bias_rows[1]).astype(jnp.bfloat16)
    head_shape = (image_count, seq_len, local_heads, HD)
    scores = (
        jnp.einsum(
            "bqhd,bkhd->bhqk",
            queries.reshape(head_shape),
            key_rows.reshape(head_shape),
            preferred_element_type=jnp.float32,
        )
        * score_scale
    )
    row_max = jnp.max(scores, axis=-1, keepdims=True)
    exp_scores = jnp.exp(scores - row_max)
    row_total = jnp.sum(exp_scores, axis=-1, keepdims=True)
    attn_probs = (exp_scores / row_total).astype(jnp.bfloat16)
    log_total = row_max + jnp.log(row_total)
    context = jnp.einsum(
        "bhqk,bkhd->bqhd",
        attn_probs,
        values.reshape(head_shape),
        preferred_element_type=jnp.float32,
    )
    context = context.astype(jnp.bfloat16).reshape(-1, local_heads * HD)
    attn_term = jnp.dot(context, out_weight, preferred_element_type=jnp.float32)
    hidden = token_rows + lax.psum(attn_term, "tensor") + shift_rows[1]
    normed_two = norm_forward(hidden, gain_rows[1], shift_rows[2])[0].astype(jnp.bfloat16)
    pre_act = jnp.dot(normed_two, up_weight, preferred_element_type=jnp.float32) + up_bias.astype(
        jnp.float32
    )
    active = gelu_value(pre_act).astype(jnp.bfloat16)
    mlp_term = jnp.dot(active, down_weight, preferred_element_type=jnp.float32)
    output_low = (hidden + lax.psum(mlp_term, "tensor") + shift_rows[3]).astype(jnp.bfloat16)
    stored = (
        layer_input,
        normed_one,
        queries,
        key_rows,
        values,
        log_total,
        context,
        hidden,
        normed_two,
        pre_act,
        active,
    )
    return (output_low, stored)


def layer_backward(grad_output, stored, weights):
    qkv_weight, out_weight, up_weight, down_weight, gains, shifts = weights
    (
        layer_input,
        normed_one,
        queries,
        key_rows,
        values,
        log_total,
        context,
        hidden,
        normed_two,
        pre_act,
        active,
    ) = stored
    image_count, seq_len, model_width = layer_input.shape
    local_heads = qkv_weight.shape[2] // HD
    score_scale = HD ** (-0.5)
    gain_rows = gains.astype(jnp.float32)
    shift_rows = shifts.astype(jnp.float32)
    grad_mix = grad_output.astype(jnp.bfloat16)
    grad_down = jnp.einsum("tf,td->fd", active, grad_mix, preferred_element_type=jnp.float32)
    grad_active = jnp.einsum("td,fd->tf", grad_mix, down_weight, preferred_element_type=jnp.float32)
    grad_pre = (grad_active * gelu_slope(pre_act)).astype(jnp.bfloat16)
    grad_up = jnp.einsum("td,tf->df", normed_two, grad_pre, preferred_element_type=jnp.float32)
    up_bias_grad = jnp.sum(grad_pre.astype(jnp.float32), axis=0)
    two_term = jnp.einsum("tf,df->td", grad_pre, up_weight, preferred_element_type=jnp.float32)
    centred_two, inverse_two = norm_forward(hidden, gain_rows[1], shift_rows[2])[1:]
    grad_normed_two = lax.psum(two_term, "tensor")
    from_two, gain_two_grad, shift_two_grad = norm_backward(
        grad_normed_two, centred_two, inverse_two, gain_rows[1]
    )
    grad_hidden = grad_output + from_two
    grad_attn = grad_hidden.astype(jnp.bfloat16)
    attn_shift_grad = jnp.sum(grad_attn.astype(jnp.float32), axis=0)
    mix_shift_grad = jnp.sum(grad_mix.astype(jnp.float32), axis=0)
    grad_out = jnp.einsum("te,td->ed", context, grad_attn, preferred_element_type=jnp.float32)
    grad_context = jnp.einsum(
        "td,ed->te", grad_attn, out_weight, preferred_element_type=jnp.float32
    ).astype(jnp.bfloat16)
    head_shape = (image_count, seq_len, local_heads, HD)
    query_heads = queries.reshape(head_shape)
    key_heads = key_rows.reshape(head_shape)
    value_heads = values.reshape(head_shape)
    context_grads = grad_context.reshape(head_shape)
    scores = (
        jnp.einsum("bqhd,bkhd->bhqk", query_heads, key_heads, preferred_element_type=jnp.float32)
        * score_scale
    )
    probs_full = jnp.exp(scores - log_total)
    mixed = jnp.einsum(
        "bqhd,bkhd->bhqk", context_grads, value_heads, preferred_element_type=jnp.float32
    )
    row_delta = jnp.sum(mixed * probs_full, axis=-1, keepdims=True)
    grad_scores = (probs_full * (mixed - row_delta)).astype(jnp.bfloat16)
    grad_values = jnp.einsum(
        "bhqk,bqhd->bkhd",
        probs_full.astype(jnp.bfloat16),
        context_grads,
        preferred_element_type=jnp.float32,
    ).astype(jnp.bfloat16)
    grad_queries = (
        jnp.einsum("bhqk,bkhd->bqhd", grad_scores, key_heads, preferred_element_type=jnp.float32)
        * score_scale
    ).astype(jnp.bfloat16)
    grad_keys = (
        jnp.einsum("bhqk,bqhd->bkhd", grad_scores, query_heads, preferred_element_type=jnp.float32)
        * score_scale
    ).astype(jnp.bfloat16)
    flat_shape = (-1, local_heads * HD)
    grad_proj = jnp.stack(
        [
            grad_queries.reshape(flat_shape),
            grad_keys.reshape(flat_shape),
            grad_values.reshape(flat_shape),
        ]
    )
    grad_qkv = jnp.einsum("td,cte->cde", normed_one, grad_proj, preferred_element_type=jnp.float32)
    qv_bias_grad = jnp.stack(
        [
            jnp.sum(grad_proj[0].astype(jnp.float32), axis=0),
            jnp.sum(grad_proj[2].astype(jnp.float32), axis=0),
        ]
    )
    one_term = jnp.einsum("cte,cde->td", grad_proj, qkv_weight, preferred_element_type=jnp.float32)
    token_rows = layer_input.astype(jnp.float32).reshape(-1, model_width)
    grad_normed_one = lax.psum(one_term, "tensor")
    centred_one, inverse_one = norm_forward(token_rows, gain_rows[0], shift_rows[0])[1:]
    from_one, gain_one_grad, shift_one_grad = norm_backward(
        grad_normed_one, centred_one, inverse_one, gain_rows[0]
    )
    grad_low = (grad_hidden + from_one).astype(jnp.bfloat16)
    grad_gains = jnp.stack([gain_one_grad, gain_two_grad])
    grad_shifts = jnp.stack([shift_one_grad, attn_shift_grad, shift_two_grad, mix_shift_grad])
    return (
        grad_low,
        (grad_qkv, grad_out, grad_up, grad_down, grad_gains, grad_shifts),
        (qv_bias_grad, up_bias_grad),
    )


def per_device(
    images,
    cotangent,
    qkv_weight,
    qv_bias,
    out_weight,
    up_weight,
    up_bias,
    down_weight,
    gains,
    shifts,
):
    micro_count, image_count, seq_len, model_width = images.shape
    section_index = lax.axis_index("section")
    local_qv = qv_bias[0]
    local_up = up_bias[0]
    weights = (
        lax.all_gather(qkv_weight[0], "fsdp", axis=1, tiled=True),
        lax.all_gather(out_weight[0], "fsdp", axis=1, tiled=True),
        lax.all_gather(up_weight[0], "fsdp", axis=0, tiled=True),
        lax.all_gather(down_weight[0], "fsdp", axis=1, tiled=True),
        lax.all_gather(gains[0], "fsdp", axis=1, tiled=True),
        lax.all_gather(shifts[0], "fsdp", axis=1, tiled=True),
    )

    def forward_tick(carried, tick_index):
        own_input = lax.dynamic_index_in_dim(
            images, jnp.minimum(tick_index, micro_count - 1), 0, keepdims=False
        )
        layer_input = jnp.where(section_index == 0, own_input, carried)
        output_low, stored = layer_forward(layer_input, weights, local_qv, local_up)
        output_low = output_low.reshape(image_count, seq_len, model_width)
        passed = from_behind(output_low, "section", 1)
        return (passed, (output_low, stored))

    ticks = jnp.arange(micro_count + 1, dtype=jnp.int32)
    output_all, stored_all = lax.scan(forward_tick, jnp.zeros_like(images[0]), ticks)[1]
    section_outputs = lax.dynamic_slice_in_dim(output_all, section_index, micro_count, 0)
    start_sums = tuple((jnp.zeros(item.shape, jnp.float32) for item in weights))
    start_biases = (jnp.zeros(local_qv.shape, jnp.float32), jnp.zeros(local_up.shape, jnp.float32))

    def backward_tick(carry, tick_index):
        received, grad_sums, bias_totals = carry
        micro_index = micro_count - tick_index - section_index
        is_valid = (micro_index >= 0) & (micro_index < micro_count)
        safe_index = jnp.clip(micro_index, 0, micro_count - 1)
        own_grad = (
            lax.dynamic_index_in_dim(cotangent, safe_index, 0, keepdims=False)
            .astype(jnp.float32)
            .reshape(-1, model_width)
        )
        grad_output = jnp.where(section_index == 1, own_grad, received)
        stored = tuple(
            (
                lax.dynamic_index_in_dim(item, safe_index + section_index, 0, keepdims=False)
                for item in stored_all
            )
        )
        grad_low, grads, biases = layer_backward(grad_output, stored, weights)
        grads = tuple((jnp.where(is_valid, item, 0.0) for item in grads))
        biases = tuple((jnp.where(is_valid, item, 0.0) for item in biases))
        grad_low = grad_low.reshape(image_count, seq_len, model_width)
        passed = from_behind(grad_low, "section", -1).astype(jnp.float32).reshape(-1, model_width)
        grad_sums = tuple((first + second for first, second in zip(grad_sums, grads)))
        bias_totals = tuple((first + second for first, second in zip(bias_totals, biases)))
        return ((passed, grad_sums, bias_totals), grad_low)

    start_grad = jnp.zeros((image_count * seq_len, model_width), jnp.float32)
    finished, grad_all = lax.scan(backward_tick, (start_grad, start_sums, start_biases), ticks)
    grad_sums, bias_totals = (finished[1], finished[2])
    final_grads = (
        lax.psum_scatter(
            grad_sums[0].astype(jnp.bfloat16), "fsdp", scatter_dimension=1, tiled=True
        ).astype(jnp.float32),
        lax.psum_scatter(
            grad_sums[1].astype(jnp.bfloat16), "fsdp", scatter_dimension=1, tiled=True
        ).astype(jnp.float32),
        lax.psum_scatter(
            grad_sums[2].astype(jnp.bfloat16), "fsdp", scatter_dimension=0, tiled=True
        ).astype(jnp.float32),
        lax.psum_scatter(
            grad_sums[3].astype(jnp.bfloat16), "fsdp", scatter_dimension=1, tiled=True
        ).astype(jnp.float32),
        lax.psum_scatter(
            grad_sums[4].astype(jnp.bfloat16), "fsdp", scatter_dimension=1, tiled=True
        ).astype(jnp.float32),
        lax.psum_scatter(
            grad_sums[5].astype(jnp.bfloat16), "fsdp", scatter_dimension=1, tiled=True
        ).astype(jnp.float32),
    )
    final_biases = lax.psum((bias_totals[0], bias_totals[1]), "fsdp")
    gain_grads, shift_grads = (final_grads[4], final_grads[5])
    input_grads = jnp.flip(lax.dynamic_slice_in_dim(grad_all, 1 - section_index, micro_count, 0), 0)
    return (
        section_outputs[None],
        input_grads[None],
        final_grads[0][None],
        final_biases[0][None],
        final_grads[1][None],
        final_grads[2][None],
        final_biases[1][None],
        final_grads[3][None],
        gain_grads[None],
        shift_grads[None],
    )


def solution(mesh):
    return jax.shard_map(
        per_device,
        mesh=mesh,
        in_specs=(
            P(None, "fsdp", None, None),
            P(None, "fsdp", None, None),
            P("section", None, "fsdp", "tensor"),
            P("section", None, "tensor"),
            P("section", "tensor", "fsdp"),
            P("section", "fsdp", "tensor"),
            P("section", "tensor"),
            P("section", "tensor", "fsdp"),
            P("section", None, "fsdp"),
            P("section", None, "fsdp"),
        ),
        out_specs=(
            P("section", None, "fsdp", None, None),
            P("section", None, "fsdp", None, None),
            P("section", None, "fsdp", "tensor"),
            P("section", None, "tensor"),
            P("section", "tensor", "fsdp"),
            P("section", "fsdp", "tensor"),
            P("section", "tensor"),
            P("section", "tensor", "fsdp"),
            P("section", None, "fsdp"),
            P("section", None, "fsdp"),
        ),
        check_vma=False,
    )
```

profile of v0, /device:TPU:0, one launch (start us, length us, event | category | flops | bytes accessed | tf_op | source)
XLA Modules:
  0.0 2444.3 jit_solution(16826438468239682339)
XLA Ops:
  12.3 19.3 all-gather.3
  35.5 12.4 all-gather
  51.0 8.1 all-gather.1
  83.8 22.2 all-gather.12.cloned.1.call-done
  112.5 1034.5 %while.66 = (s32[]{:T(128)}, bf16[1,729,1152]{2,1,0:T(8,128)(2,1)}, bf16[3,1,729,1152]{3,2,1,0:T(8,128)(2,1)}, bf16[3,1,729,1152]{3,2,1,0:T(8,128)(2,1)}, bf16[3...) while((s32[]{:T(128)}, bf16[1,729,1152]{2,1,0:T(8,128)(2,1)}, ...), condition=%wide.region_9.10_spmd, body=%wide.region_0.9_spmd.sunk | while | flops 6232035840 | bytes 263704656 | solution.py:247
  145.6 130.7 %all-reduce.6.cloned.1.call-done = f32[729,1152]{1,0:T(8,128)} async-done(((f32[729,1152]{1,0:T(8,128)}), f32[729,1152]{1,0:T(8,128)}) %all-reduce.6.cloned.1.call-update) | async-done | bytes 3359248 | tf_op jit(solution)/shard_map/while/body/eval_jaxpr/psum | solution.py:86
  297.6 124.3 %all-reduce.8.cloned.1.call-done = f32[729,1152]{1,0:T(8,128)} async-done(((f32[729,1152]{1,0:T(8,128)}), f32[729,1152]{1,0:T(8,128)}) %all-reduce.8.cloned.1.call-update) | async-done | bytes 3359248 | tf_op jit(solution)/shard_map/while/body/eval_jaxpr/psum | solution.py:93
  436.2 29.8 %collective-permute-done = bf16[1,729,1152]{2,1,0:T(8,128)(2,1)} collective-permute-done((bf16[1,729,1152]{2,1,0:T(8,128)(2,1)}, bf16[1,729,1152]{2,1,0:T(8,128)(2,1)}, u32[]{:S(2)}, u32[]{:S(2)}) %collective-permute-start) | collective-permute-done | bytes 1679648 | tf_op jit(solution)/shard_map/while/body/eval_jaxpr/ppermute | solution.py:15
  486.1 130.8 %all-reduce.6.cloned.1.call-done = f32[729,1152]{1,0:T(8,128)} async-done(((f32[729,1152]{1,0:T(8,128)}), f32[729,1152]{1,0:T(8,128)}) %all-reduce.6.cloned.1.call-update) | async-done | bytes 3359248 | tf_op jit(solution)/shard_map/while/body/eval_jaxpr/psum | solution.py:86
  638.1 124.4 %all-reduce.8.cloned.1.call-done = f32[729,1152]{1,0:T(8,128)} async-done(((f32[729,1152]{1,0:T(8,128)}), f32[729,1152]{1,0:T(8,128)}) %all-reduce.8.cloned.1.call-update) | async-done | bytes 3359248 | tf_op jit(solution)/shard_map/while/body/eval_jaxpr/psum | solution.py:93
  776.8 29.7 %collective-permute-done = bf16[1,729,1152]{2,1,0:T(8,128)(2,1)} collective-permute-done((bf16[1,729,1152]{2,1,0:T(8,128)(2,1)}, bf16[1,729,1152]{2,1,0:T(8,128)(2,1)}, u32[]{:S(2)}, u32[]{:S(2)}) %collective-permute-start) | collective-permute-done | bytes 1679648 | tf_op jit(solution)/shard_map/while/body/eval_jaxpr/ppermute | solution.py:15
  826.6 130.8 %all-reduce.6.cloned.1.call-done = f32[729,1152]{1,0:T(8,128)} async-done(((f32[729,1152]{1,0:T(8,128)}), f32[729,1152]{1,0:T(8,128)}) %all-reduce.6.cloned.1.call-update) | async-done | bytes 3359248 | tf_op jit(solution)/shard_map/while/body/eval_jaxpr/psum | solution.py:86
  978.7 124.3 %all-reduce.8.cloned.1.call-done = f32[729,1152]{1,0:T(8,128)} async-done(((f32[729,1152]{1,0:T(8,128)}), f32[729,1152]{1,0:T(8,128)}) %all-reduce.8.cloned.1.call-update) | async-done | bytes 3359248 | tf_op jit(solution)/shard_map/while/body/eval_jaxpr/psum | solution.py:93
  1117.1 29.7 %collective-permute-done = bf16[1,729,1152]{2,1,0:T(8,128)(2,1)} collective-permute-done((bf16[1,729,1152]{2,1,0:T(8,128)(2,1)}, bf16[1,729,1152]{2,1,0:T(8,128)(2,1)}, u32[]{:S(2)}, u32[]{:S(2)}) %collective-permute-start) | collective-permute-done | bytes 1679648 | tf_op jit(solution)/shard_map/while/body/eval_jaxpr/ppermute | solution.py:15
  1149.9 1104.1 %while.67 = (s32[]{:T(128)}, f32[729,1152]{1,0:T(8,128)S(1)}, f32[3,1152,288]{1,2,0:T(8,128)}, f32[288,1152]{1,0:T(8,128)}, f32[1152,1076]{0,1:T(8,128)}, /*inde...) while((s32[]{:T(128)}, f32[729,1152]{1,0:T(8,128)S(1)}, ...), condition=%wide.region_31.32_spmd.clone, body=%wide.region_10.31_spmd.clone.sunk | while | flops 12738733056 | bytes 490833920 | solution.py:279
  1200.5 115.7 %all-reduce.10.cloned.1.call-done = f32[729,1152]{1,0:T(8,128)} async-done(((f32[729,1152]{1,0:T(8,128)}), f32[729,1152]{1,0:T(8,128)}) %all-reduce.10.cloned.1.call-update) | async-done | bytes 3359248 | tf_op jit(solution)/shard_map/while/body/eval_jaxpr/psum | solution.py:138
  1331.7 10.2 multiply_convert_fusion.2
  1378.7 106.2 %all-reduce.12.cloned.1.call-done = f32[729,1152]{1,0:T(8,128)} async-done(((f32[729,1152]{1,0:T(8,128)}), f32[729,1152]{1,0:T(8,128)}) %all-reduce.12.cloned.1.call-update) | async-done | bytes 3359248 | tf_op jit(solution)/shard_map/while/body/eval_jaxpr/psum | solution.py:196
  1498.5 34.7 %collective-permute-done.1 = bf16[1,729,1152]{2,1,0:T(8,128)(2,1)S(1)} collective-permute-done((bf16[1,729,1152]{2,1,0:T(8,128)(2,1)S(1)}, bf16[1,729,1152]{2,1,0:T(8,128)(2,1)S(1)}, u32[]{:S(2)}, u32[]{:S(2)}) %collective-permute-start.1) | collective-permute-done | bytes 1679648 | tf_op jit(solution)/shard_map/while/body/eval_jaxpr/ppermute | solution.py:15
  1562.8 113.6 %all-reduce.10.cloned.1.call-done = f32[729,1152]{1,0:T(8,128)} async-done(((f32[729,1152]{1,0:T(8,128)}), f32[729,1152]{1,0:T(8,128)}) %all-reduce.10.cloned.1.call-update) | async-done | bytes 3359248 | tf_op jit(solution)/shard_map/while/body/eval_jaxpr/psum | solution.py:138
  1691.9 10.2 multiply_convert_fusion.2
  1722.2 7.7 fusion.215
  1740.9 104.2 %all-reduce.12.cloned.1.call-done = f32[729,1152]{1,0:T(8,128)} async-done(((f32[729,1152]{1,0:T(8,128)}), f32[729,1152]{1,0:T(8,128)}) %all-reduce.12.cloned.1.call-update) | async-done | bytes 3359248 | tf_op jit(solution)/shard_map/while/body/eval_jaxpr/psum | solution.py:196
  1858.7 34.7 %collective-permute-done.1 = bf16[1,729,1152]{2,1,0:T(8,128)(2,1)S(1)} collective-permute-done((bf16[1,729,1152]{2,1,0:T(8,128)(2,1)S(1)}, bf16[1,729,1152]{2,1,0:T(8,128)(2,1)S(1)}, u32[]{:S(2)}, u32[]{:S(2)}) %collective-permute-start.1) | collective-permute-done | bytes 1679648 | tf_op jit(solution)/shard_map/while/body/eval_jaxpr/ppermute | solution.py:15
  1922.9 113.6 %all-reduce.10.cloned.1.call-done = f32[729,1152]{1,0:T(8,128)} async-done(((f32[729,1152]{1,0:T(8,128)}), f32[729,1152]{1,0:T(8,128)}) %all-reduce.10.cloned.1.call-update) | async-done | bytes 3359248 | tf_op jit(solution)/shard_map/while/body/eval_jaxpr/psum | solution.py:138
  2051.8 10.2 multiply_convert_fusion.2
  2100.9 104.2 %all-reduce.12.cloned.1.call-done = f32[729,1152]{1,0:T(8,128)} async-done(((f32[729,1152]{1,0:T(8,128)}), f32[729,1152]{1,0:T(8,128)}) %all-reduce.12.cloned.1.call-update) | async-done | bytes 3359248 | tf_op jit(solution)/shard_map/while/body/eval_jaxpr/psum | solution.py:196
  2218.7 34.7 %collective-permute-done.1 = bf16[1,729,1152]{2,1,0:T(8,128)(2,1)S(1)} collective-permute-done((bf16[1,729,1152]{2,1,0:T(8,128)(2,1)S(1)}, bf16[1,729,1152]{2,1,0:T(8,128)(2,1)S(1)}, u32[]{:S(2)}, u32[]{:S(2)}) %collective-permute-start.1) | collective-permute-done | bytes 1679648 | tf_op jit(solution)/shard_map/while/body/eval_jaxpr/ppermute | solution.py:15
  2296.5 31.6 %rev.4 = bf16[2,1,729,1152]{3,0,2,1:T(2,128)(2,1)} reverse(bf16[2,1,729,1152]{3,0,2,1:T(2,128)(2,1)} %constant_dynamic-slice_fusion.3), dimensions={0} | reverse | bytes 6718464 | tf_op jit(solution)/shard_map/jit(_flip)/rev | solution.py:303
  2346.4 13.1 reduce-scatter.19.cloned.1.call-done
  2364.7 32.0 %reduce-scatter.23.cloned.1.call-done = bf16[288,1076]{1,0:T(8,128)(2,1)} async-done(((bf16[1152,1076]{1,0:T(8,128)(2,1)}), bf16[288,1076]{1,0:T(8,128)(2,1)}) %reduce-scatter.23.cloned.1.call-update) | async-done | bytes 619792
  2399.9 34.1 %reduce-scatter.25.cloned.1.call-done = bf16[288,1076]{1,0:T(8,128)(2,1)} async-done(((bf16[1152,1076]{1,0:T(8,128)(2,1)}), bf16[288,1076]{1,0:T(8,128)(2,1)}) %reduce-scatter.25.cloned.1.call-update) | async-done | bytes 619792
  (790 shorter events, 560.3 us)
Async XLA Ops:
  7.2 58.4 %all-gather.10.cloned.1.call-start = ((), (), s32[]{:S(2)}) async-start(), calls=%async_computation.6 | async-start | bytes 4423680 | tf_op jit(solution)/shard_map/all_gather | solution.py:228
  9.8 68.9 %all-gather.14.cloned.1.call-start = ((), (), s32[]{:S(2)}) async-start(), calls=%async_computation.8 | async-start | bytes 3317760 | tf_op jit(solution)/shard_map/all_gather | solution.py:231
  10.5 95.4 %all-gather.12.cloned.1.call-start = ((), (), s32[]{:S(2)}) async-start(), calls=%async_computation.7 | async-start | bytes 3317760 | tf_op jit(solution)/shard_map/all_gather | solution.py:230
  125.5 150.8 %all-reduce.6.cloned.1.call-start = ((), (), s32[]{:S(2)}) async-start(), calls=%async_computation.15 | async-start | bytes 6782976 | tf_op jit(solution)/shard_map/while/body/eval_jaxpr/psum | solution.py:86
  142.6 133.7 %copy-start.42 = (f32[1152]{0:T(1024)S(1)}, f32[1152]{0:T(1024)}, u32[]{:S(2)}) copy-start(f32[1152]{0:T(1024)} %get-tuple-element.1532) | copy-start | bytes 13828 | tf_op jit(solution)/shard_map/while
  145.5 276.4 %all-reduce.8.cloned.1.call-start = ((), (), s32[]{:S(2)}) async-start(), calls=%async_computation.16 | async-start | bytes 6782976 | tf_op jit(solution)/shard_map/while/body/eval_jaxpr/psum | solution.py:93
  426.2 39.8 %collective-permute-start = (bf16[1,729,1152]{2,1,0:T(8,128)(2,1)}, bf16[1,729,1152]{2,1,0:T(8,128)(2,1)}, u32[]{:S(2)}, u32[]{:S(2)}) collective-permute-start(bf16[1,729,1152]{2,1,0:T(8,128)(2,1)} %bitcast.319), channel_id=1, source_target_pairs={{0,16},{1,17},{2,18},{3,19},{4,20},{5,21},{6,22},{7,23},{8,24},{9,... | collective-permute-start | bytes 5038856 | tf_op jit(solution)/shard_map/while/body/eval_jaxpr/ppermute | solution.py:15
  466.0 150.8 %all-reduce.6.cloned.1.call-start = ((), (), s32[]{:S(2)}) async-start(), calls=%async_computation.15 | async-start | bytes 6782976 | tf_op jit(solution)/shard_map/while/body/eval_jaxpr/psum | solution.py:86
  483.1 133.8 %copy-start.42 = (f32[1152]{0:T(1024)S(1)}, f32[1152]{0:T(1024)}, u32[]{:S(2)}) copy-start(f32[1152]{0:T(1024)} %get-tuple-element.1532) | copy-start | bytes 13828 | tf_op jit(solution)/shard_map/while
  486.0 276.4 %all-reduce.8.cloned.1.call-start = ((), (), s32[]{:S(2)}) async-start(), calls=%async_computation.16 | async-start | bytes 6782976 | tf_op jit(solution)/shard_map/while/body/eval_jaxpr/psum | solution.py:93
  634.1 128.4 %copy-start.43 = (f32[1152]{0:T(1024)S(1)}, f32[1152]{0:T(1024)}, u32[]{:S(2)}) copy-start(f32[1152]{0:T(1024)} %get-tuple-element.1531) | copy-start | bytes 13828 | tf_op jit(solution)/shard_map/while
  766.7 39.8 %collective-permute-start = (bf16[1,729,1152]{2,1,0:T(8,128)(2,1)}, bf16[1,729,1152]{2,1,0:T(8,128)(2,1)}, u32[]{:S(2)}, u32[]{:S(2)}) collective-permute-start(bf16[1,729,1152]{2,1,0:T(8,128)(2,1)} %bitcast.319), channel_id=1, source_target_pairs={{0,16},{1,17},{2,18},{3,19},{4,20},{5,21},{6,22},{7,23},{8,24},{9,... | collective-permute-start | bytes 5038856 | tf_op jit(solution)/shard_map/while/body/eval_jaxpr/ppermute | solution.py:15
  806.5 150.8 %all-reduce.6.cloned.1.call-start = ((), (), s32[]{:S(2)}) async-start(), calls=%async_computation.15 | async-start | bytes 6782976 | tf_op jit(solution)/shard_map/while/body/eval_jaxpr/psum | solution.py:86
  823.6 133.8 %copy-start.42 = (f32[1152]{0:T(1024)S(1)}, f32[1152]{0:T(1024)}, u32[]{:S(2)}) copy-start(f32[1152]{0:T(1024)} %get-tuple-element.1532) | copy-start | bytes 13828 | tf_op jit(solution)/shard_map/while
  826.5 276.4 %all-reduce.8.cloned.1.call-start = ((), (), s32[]{:S(2)}) async-start(), calls=%async_computation.16 | async-start | bytes 6782976 | tf_op jit(solution)/shard_map/while/body/eval_jaxpr/psum | solution.py:93
  974.6 128.4 %copy-start.43 = (f32[1152]{0:T(1024)S(1)}, f32[1152]{0:T(1024)}, u32[]{:S(2)}) copy-start(f32[1152]{0:T(1024)} %get-tuple-element.1531) | copy-start | bytes 13828 | tf_op jit(solution)/shard_map/while
  1107.1 39.8 %collective-permute-start = (bf16[1,729,1152]{2,1,0:T(8,128)(2,1)}, bf16[1,729,1152]{2,1,0:T(8,128)(2,1)}, u32[]{:S(2)}, u32[]{:S(2)}) collective-permute-start(bf16[1,729,1152]{2,1,0:T(8,128)(2,1)} %bitcast.319), channel_id=1, source_target_pairs={{0,16},{1,17},{2,18},{3,19},{4,20},{5,21},{6,22},{7,23},{8,24},{9,... | collective-permute-start | bytes 5038856 | tf_op jit(solution)/shard_map/while/body/eval_jaxpr/ppermute | solution.py:15
  1171.3 144.9 %all-reduce.10.cloned.1.call-start = ((), (), s32[]{:S(2)}) async-start(), calls=%async_computation.17 | async-start | bytes 6782976 | tf_op jit(solution)/shard_map/while/body/eval_jaxpr/psum | solution.py:138
  1186.8 298.1 %all-reduce.12.cloned.1.call-start = ((), (), s32[]{:S(2)}) async-start(), calls=%async_computation.18 | async-start | bytes 6782976 | tf_op jit(solution)/shard_map/while/body/eval_jaxpr/psum | solution.py:196
  1492.7 40.5 %collective-permute-start.1 = (bf16[1,729,1152]{2,1,0:T(8,128)(2,1)S(1)}, bf16[1,729,1152]{2,1,0:T(8,128)(2,1)S(1)}, u32[]{:S(2)}, u32[]{:S(2)}) collective-permute-start(bf16[1,729,1152]{2,1,0:T(8,128)(2,1)S(1)} %bitcast.382), channel_id=1, source_target_pairs={{16,0},{17,1},{18,2},{19,3},{20,4},{21,5},{22,6},{23,7},{24,8},{25... | collective-permute-start | bytes 5038856 | tf_op jit(solution)/shard_map/while/body/eval_jaxpr/ppermute | solution.py:15
  1533.4 143.0 %all-reduce.10.cloned.1.call-start = ((), (), s32[]{:S(2)}) async-start(), calls=%async_computation.17 | async-start | bytes 6782976 | tf_op jit(solution)/shard_map/while/body/eval_jaxpr/psum | solution.py:138
  1548.9 296.2 %all-reduce.12.cloned.1.call-start = ((), (), s32[]{:S(2)}) async-start(), calls=%async_computation.18 | async-start | bytes 6782976 | tf_op jit(solution)/shard_map/while/body/eval_jaxpr/psum | solution.py:196
  1852.9 40.5 %collective-permute-start.1 = (bf16[1,729,1152]{2,1,0:T(8,128)(2,1)S(1)}, bf16[1,729,1152]{2,1,0:T(8,128)(2,1)S(1)}, u32[]{:S(2)}, u32[]{:S(2)}) collective-permute-start(bf16[1,729,1152]{2,1,0:T(8,128)(2,1)S(1)} %bitcast.382), channel_id=1, source_target_pairs={{16,0},{17,1},{18,2},{19,3},{20,4},{21,5},{22,6},{23,7},{24,8},{25... | collective-permute-start | bytes 5038856 | tf_op jit(solution)/shard_map/while/body/eval_jaxpr/ppermute | solution.py:15
  1893.6 143.0 %all-reduce.10.cloned.1.call-start = ((), (), s32[]{:S(2)}) async-start(), calls=%async_computation.17 | async-start | bytes 6782976 | tf_op jit(solution)/shard_map/while/body/eval_jaxpr/psum | solution.py:138
  1909.1 296.0 %all-reduce.12.cloned.1.call-start = ((), (), s32[]{:S(2)}) async-start(), calls=%async_computation.18 | async-start | bytes 6782976 | tf_op jit(solution)/shard_map/while/body/eval_jaxpr/psum | solution.py:196
  2212.9 40.5 %collective-permute-start.1 = (bf16[1,729,1152]{2,1,0:T(8,128)(2,1)S(1)}, bf16[1,729,1152]{2,1,0:T(8,128)(2,1)S(1)}, u32[]{:S(2)}, u32[]{:S(2)}) collective-permute-start(bf16[1,729,1152]{2,1,0:T(8,128)(2,1)S(1)} %bitcast.382), channel_id=1, source_target_pairs={{16,0},{17,1},{18,2},{19,3},{20,4},{21,5},{22,6},{23,7},{24,8},{25... | collective-permute-start | bytes 5038856 | tf_op jit(solution)/shard_map/while/body/eval_jaxpr/ppermute | solution.py:15
  2254.0 87.3 %reduce-scatter.27.cloned.1.call-start = ((), (), s32[]{:S(2)}) async-start(), calls=%async_computation.13 | async-start | bytes 368640
  2255.0 87.9 %reduce-scatter.29.cloned.1.call-start = ((), (), s32[]{:S(2)}) async-start(), calls=%async_computation.14 | async-start | bytes 368640
  2256.0 88.4 %reduce-scatter.21.cloned.1.call-start = ((), (), s32[]{:S(2)}) async-start(), calls=%async_computation.10 | async-start | bytes 1105920
  2258.7 100.9 %reduce-scatter.19.cloned.1.call-start = ((), (), s32[]{:S(2)}) async-start(), calls=%async_computation.9 | async-start | bytes 2580480
  2272.6 124.2 %reduce-scatter.23.cloned.1.call-start = ((), (), s32[]{:S(2)}) async-start(), calls=%async_computation.11 | async-start | bytes 3317760
  2278.6 155.4 %reduce-scatter.25.cloned.1.call-start = ((), (), s32[]{:S(2)}) async-start(), calls=%async_computation.12 | async-start | bytes 3317760
  (202 other events, 1413.2 us)
Sparse Core Ops, SparseCore 0:
  10.1 40.3 all-gather.9
  52.1 26.5 all-gather.13
  80.2 25.7 all-gather.11
  145.7 130.6 all-reduce.5
  293.7 128.1 all-reduce.7
  486.1 130.6 all-reduce.5
  634.2 128.1 all-reduce.7
  826.7 130.6 all-reduce.5
  974.8 128.1 all-reduce.7
  1186.9 129.2 all-reduce.9
  1357.6 127.2 all-reduce.11
  1549.1 127.3 all-reduce.9
  1717.8 127.2 all-reduce.11
  1909.2 127.3 all-reduce.9
  2077.8 127.2 all-reduce.11
  2257.6 18.3 reduce-scatter.26
  2278.9 20.2 reduce-scatter.28
  2302.2 23.7 reduce-scatter.20
  2328.6 30.9 reduce-scatter.18
  2362.0 34.7 reduce-scatter.22
  2399.3 34.7 reduce-scatter.24
where the time goes:
time: 2450 us; the launch traced here: 2440 us
  waiting for transfers between devices  1730 us (71%)
  matrix products  218 us (9%)
  other arithmetic  196 us (8%)
  local copies, waits for them, and re-layouts  184 us (8%)
  blocking collectives  46.4 us (2%)
  loops' own time  41.8 us (2%)
    psum x3, waiting for transfers between devices, layer_forward(): hidden = token_rows + lax.psum(attn_term, 'tensor') + shift_rows[1]  392 us
    psum x3, waiting for transfers between devices, layer_forward(): lax.psum(mlp_term, 'tensor')  373 us
    psum x3, waiting for transfers between devices, layer_backward(): grad_normed_two = lax.psum(two_term, 'tensor')  343 us
    psum x3, waiting for transfers between devices, layer_backward(): grad_normed_one = lax.psum(one_term, 'tensor')  315 us
    ppermute x6, waiting for transfers between devices, from_behind(): lax.ppermute(value, axis, [(source, source + steps) for source in range(l...  193 us
    unnamed x15, waiting for transfers between devices  80.8 us
    dynamic_update_slice x27, other arithmetic, per_device(): lax.scan(forward_tick, jnp.zeros_like(images[0]), ticks)[1]  69.8 us
  transfers between devices with their start and end apart: 27, of which 23 were waited for; matrix products, arithmetic and copies ran while one was open for 11% of the time, Pallas kernels for 0%

commit v1 on v0

--- a/solution.py
+++ b/solution.py
@@ -7,6 +7,7 @@
 NORM_EPS = 1e-06
 GELU_ROOT = 0.7978845608028654
 GELU_CUBIC = 0.044715
+obtain_entries_over_axis = lambda slab_in: jnp.sum(lax.all_gather(slab_in, "tensor"), axis=0)
 
 
 def from_behind(value, axis, steps):
@@ -135,7 +136,7 @@
     up_bias_grad = jnp.sum(grad_pre.astype(jnp.float32), axis=0)
     two_term = jnp.einsum("tf,df->td", grad_pre, up_weight, preferred_element_type=jnp.float32)
     centred_two, inverse_two = norm_forward(hidden, gain_rows[1], shift_rows[2])[1:]
-    grad_normed_two = lax.psum(two_term, "tensor")
+    grad_normed_two = obtain_entries_over_axis(two_term)
     from_two, gain_two_grad, shift_two_grad = norm_backward(
         grad_normed_two, centred_two, inverse_two, gain_rows[1]
     )

time: 2450 us -> 2790 us (1.14)
  waiting for transfers between devices: 1730 us -> 2030 us
    all_gather x0 -> x3, waiting for transfers between devices: none -> 655 us  [lax.all_gather(slab_in, 'tensor')]
    psum x3 -> x0, waiting for transfers between devices: 343 us -> none  [layer_backward(): grad_normed_two = lax.psum(two_term, 'tensor')]
  transfers between devices with their start and end apart: 27 -> 27, of which waited for: 23 -> 23; matrix products, arithmetic and copies ran while one was open for 11% -> 10% of each run, Pallas kernels for 0% -> 0%
where the time goes in v1:
time: 2790 us; the launch traced here: 2780 us
  waiting for transfers between devices  2030 us (73%)
  matrix products  220 us (8%)
  other arithmetic  216 us (8%)
  local copies, waits for them, and re-layouts  184 us (7%)
  blocking collectives  46.4 us (2%)
  loops' own time  45.3 us (2%)
    all_gather x3, waiting for transfers between devices, lax.all_gather(slab_in, 'tensor')  655 us
    psum x3, waiting for transfers between devices, layer_forward(): hidden = token_rows + lax.psum(attn_term, 'tensor') + shift_rows[1]  392 us
    psum x3, waiting for transfers between devices, layer_forward(): lax.psum(mlp_term, 'tensor')  373 us
    psum x3, waiting for transfers between devices, layer_backward(): grad_normed_one = lax.psum(one_term, 'tensor')  311 us
    ppermute x6, waiting for transfers between devices, from_behind(): lax.ppermute(value, axis, [(source, source + steps) for source in range(l...  193 us
    unnamed x15, waiting for transfers between devices  80.7 us
    dynamic_update_slice x27, other arithmetic, per_device(): lax.scan(forward_tick, jnp.zeros_like(images[0]), ticks)[1]  69.7 us
  transfers between devices with their start and end apart: 27, of which 23 were waited for; matrix products, arithmetic and copies ran while one was open for 10% of the time, Pallas kernels for 0%

profile of v1, /device:TPU:0, one launch (start us, length us, event | category | flops | bytes accessed | tf_op | source)
XLA Modules:
  0.0 2777.9 jit_solution(7784001579431533880)
XLA Ops:
  12.3 19.3 all-gather.4
  35.6 12.4 all-gather.1
  51.0 8.2 all-gather.2
  83.8 22.2 all-gather.18.cloned.1.call-done
  112.4 1034.2 %while.66 = (s32[]{:T(128)}, bf16[1,729,1152]{2,1,0:T(8,128)(2,1)}, bf16[3,1,729,1152]{3,2,1,0:T(8,128)(2,1)}, bf16[3,1,729,1152]{3,2,1,0:T(8,128)(2,1)}, bf16[3...) while((s32[]{:T(128)}, bf16[1,729,1152]{2,1,0:T(8,128)(2,1)}, ...), condition=%wide.region_9.10_spmd, body=%wide.region_0.9_spmd.sunk | while | flops 6232035840 | bytes 263704656 | solution.py:248
  145.5 130.7 %all-reduce.5.cloned.1.call-done = f32[729,1152]{1,0:T(8,128)} async-done(((f32[729,1152]{1,0:T(8,128)}), f32[729,1152]{1,0:T(8,128)}) %all-reduce.5.cloned.1.call-update) | async-done | bytes 3359248 | tf_op jit(solution)/shard_map/while/body/eval_jaxpr/psum | solution.py:87
  297.5 124.3 %all-reduce.7.cloned.1.call-done = f32[729,1152]{1,0:T(8,128)} async-done(((f32[729,1152]{1,0:T(8,128)}), f32[729,1152]{1,0:T(8,128)}) %all-reduce.7.cloned.1.call-update) | async-done | bytes 3359248 | tf_op jit(solution)/shard_map/while/body/eval_jaxpr/psum | solution.py:94
  436.1 29.7 %collective-permute-done = bf16[1,729,1152]{2,1,0:T(8,128)(2,1)} collective-permute-done((bf16[1,729,1152]{2,1,0:T(8,128)(2,1)}, bf16[1,729,1152]{2,1,0:T(8,128)(2,1)}, u32[]{:S(2)}, u32[]{:S(2)}) %collective-permute-start) | collective-permute-done | bytes 1679648 | tf_op jit(solution)/shard_map/while/body/eval_jaxpr/ppermute | solution.py:16
  486.0 130.8 %all-reduce.5.cloned.1.call-done = f32[729,1152]{1,0:T(8,128)} async-done(((f32[729,1152]{1,0:T(8,128)}), f32[729,1152]{1,0:T(8,128)}) %all-reduce.5.cloned.1.call-update) | async-done | bytes 3359248 | tf_op jit(solution)/shard_map/while/body/eval_jaxpr/psum | solution.py:87
  638.0 124.3 %all-reduce.7.cloned.1.call-done = f32[729,1152]{1,0:T(8,128)} async-done(((f32[729,1152]{1,0:T(8,128)}), f32[729,1152]{1,0:T(8,128)}) %all-reduce.7.cloned.1.call-update) | async-done | bytes 3359248 | tf_op jit(solution)/shard_map/while/body/eval_jaxpr/psum | solution.py:94
  776.6 29.7 %collective-permute-done = bf16[1,729,1152]{2,1,0:T(8,128)(2,1)} collective-permute-done((bf16[1,729,1152]{2,1,0:T(8,128)(2,1)}, bf16[1,729,1152]{2,1,0:T(8,128)(2,1)}, u32[]{:S(2)}, u32[]{:S(2)}) %collective-permute-start) | collective-permute-done | bytes 1679648 | tf_op jit(solution)/shard_map/while/body/eval_jaxpr/ppermute | solution.py:16
  826.4 130.8 %all-reduce.5.cloned.1.call-done = f32[729,1152]{1,0:T(8,128)} async-done(((f32[729,1152]{1,0:T(8,128)}), f32[729,1152]{1,0:T(8,128)}) %all-reduce.5.cloned.1.call-update) | async-done | bytes 3359248 | tf_op jit(solution)/shard_map/while/body/eval_jaxpr/psum | solution.py:87
  978.4 124.3 %all-reduce.7.cloned.1.call-done = f32[729,1152]{1,0:T(8,128)} async-done(((f32[729,1152]{1,0:T(8,128)}), f32[729,1152]{1,0:T(8,128)}) %all-reduce.7.cloned.1.call-update) | async-done | bytes 3359248 | tf_op jit(solution)/shard_map/while/body/eval_jaxpr/psum | solution.py:94
  1116.8 29.8 %collective-permute-done = bf16[1,729,1152]{2,1,0:T(8,128)(2,1)} collective-permute-done((bf16[1,729,1152]{2,1,0:T(8,128)(2,1)}, bf16[1,729,1152]{2,1,0:T(8,128)(2,1)}, u32[]{:S(2)}, u32[]{:S(2)}) %collective-permute-start) | collective-permute-done | bytes 1679648 | tf_op jit(solution)/shard_map/while/body/eval_jaxpr/ppermute | solution.py:16
  1149.6 1438.0 %while.67 = (s32[]{:T(128)}, f32[729,1152]{1,0:T(8,128)S(1)}, f32[3,1152,288]{1,2,0:T(8,128)}, f32[288,1152]{1,0:T(8,128)}, f32[1152,1076]{0,1:T(8,128)}, /*inde...) while((s32[]{:T(128)}, f32[729,1152]{1,0:T(8,128)S(1)}, ...), condition=%wide.region_31.32_spmd.clone, body=%wide.region_10.31_spmd.clone.sunk | while | flops 12742931456 | bytes 524523008 | solution.py:280
  1202.4 219.8 %all-gather.22.cloned.1.call-done = f32[4,729,1152]{2,1,0:T(8,128)} async-done(((f32[1,729,1152]{2,1,0:T(8,128)}), f32[4,729,1152]{2,1,0:T(8,128)}) %all-gather.22.cloned.1.call-update) | async-done | bytes 13436944 | tf_op jit(solution)/shard_map/while/body/eval_jaxpr/all_gather | solution.py:10
  1443.3 10.2 multiply_convert_fusion.2
  1490.9 104.8 %all-reduce.9.cloned.1.call-done = f32[729,1152]{1,0:T(8,128)} async-done(((f32[729,1152]{1,0:T(8,128)}), f32[729,1152]{1,0:T(8,128)}) %all-reduce.9.cloned.1.call-update) | async-done | bytes 3359248 | tf_op jit(solution)/shard_map/while/body/eval_jaxpr/psum | solution.py:197
  1609.3 34.7 %collective-permute-done.1 = bf16[1,729,1152]{2,1,0:T(8,128)(2,1)S(1)} collective-permute-done((bf16[1,729,1152]{2,1,0:T(8,128)(2,1)S(1)}, bf16[1,729,1152]{2,1,0:T(8,128)(2,1)S(1)}, u32[]{:S(2)}, u32[]{:S(2)}) %collective-permute-start.1) | collective-permute-done | bytes 1679648 | tf_op jit(solution)/shard_map/while/body/eval_jaxpr/ppermute | solution.py:16
  1674.7 217.7 %all-gather.22.cloned.1.call-done = f32[4,729,1152]{2,1,0:T(8,128)} async-done(((f32[1,729,1152]{2,1,0:T(8,128)}), f32[4,729,1152]{2,1,0:T(8,128)}) %all-gather.22.cloned.1.call-update) | async-done | bytes 13436944 | tf_op jit(solution)/shard_map/while/body/eval_jaxpr/all_gather | solution.py:10
  1913.6 10.2 multiply_convert_fusion.2
  1963.1 102.9 %all-reduce.9.cloned.1.call-done = f32[729,1152]{1,0:T(8,128)} async-done(((f32[729,1152]{1,0:T(8,128)}), f32[729,1152]{1,0:T(8,128)}) %all-reduce.9.cloned.1.call-update) | async-done | bytes 3359248 | tf_op jit(solution)/shard_map/while/body/eval_jaxpr/psum | solution.py:197
  2079.6 34.7 %collective-permute-done.1 = bf16[1,729,1152]{2,1,0:T(8,128)(2,1)S(1)} collective-permute-done((bf16[1,729,1152]{2,1,0:T(8,128)(2,1)S(1)}, bf16[1,729,1152]{2,1,0:T(8,128)(2,1)S(1)}, u32[]{:S(2)}, u32[]{:S(2)}) %collective-permute-start.1) | collective-permute-done | bytes 1679648 | tf_op jit(solution)/shard_map/while/body/eval_jaxpr/ppermute | solution.py:16
  2145.0 217.7 %all-gather.22.cloned.1.call-done = f32[4,729,1152]{2,1,0:T(8,128)} async-done(((f32[1,729,1152]{2,1,0:T(8,128)}), f32[4,729,1152]{2,1,0:T(8,128)}) %all-gather.22.cloned.1.call-update) | async-done | bytes 13436944 | tf_op jit(solution)/shard_map/while/body/eval_jaxpr/all_gather | solution.py:10
  2383.8 10.2 multiply_convert_fusion.2
  2414.6 7.7 fusion.215
  2433.3 102.9 %all-reduce.9.cloned.1.call-done = f32[729,1152]{1,0:T(8,128)} async-done(((f32[729,1152]{1,0:T(8,128)}), f32[729,1152]{1,0:T(8,128)}) %all-reduce.9.cloned.1.call-update) | async-done | bytes 3359248 | tf_op jit(solution)/shard_map/while/body/eval_jaxpr/psum | solution.py:197
  2549.9 34.7 %collective-permute-done.1 = bf16[1,729,1152]{2,1,0:T(8,128)(2,1)S(1)} collective-permute-done((bf16[1,729,1152]{2,1,0:T(8,128)(2,1)S(1)}, bf16[1,729,1152]{2,1,0:T(8,128)(2,1)S(1)}, u32[]{:S(2)}, u32[]{:S(2)}) %collective-permute-start.1) | collective-permute-done | bytes 1679648 | tf_op jit(solution)/shard_map/while/body/eval_jaxpr/ppermute | solution.py:16
  2630.2 31.6 %rev.4 = bf16[2,1,729,1152]{3,0,2,1:T(2,128)(2,1)} reverse(bf16[2,1,729,1152]{3,0,2,1:T(2,128)(2,1)} %constant_dynamic-slice_fusion.3), dimensions={0} | reverse | bytes 6718464 | tf_op jit(solution)/shard_map/jit(_flip)/rev | solution.py:304
  2680.1 13.0 reduce-scatter.19.cloned.1.call-done
  2698.2 32.0 %reduce-scatter.23.cloned.1.call-done = bf16[288,1076]{1,0:T(8,128)(2,1)} async-done(((bf16[1152,1076]{1,0:T(8,128)(2,1)}), bf16[288,1076]{1,0:T(8,128)(2,1)}) %reduce-scatter.23.cloned.1.call-update) | async-done | bytes 619792
  2733.4 34.1 %reduce-scatter.25.cloned.1.call-done = bf16[288,1076]{1,0:T(8,128)(2,1)} async-done(((bf16[1152,1076]{1,0:T(8,128)(2,1)}), bf16[288,1076]{1,0:T(8,128)(2,1)}) %reduce-scatter.25.cloned.1.call-update) | async-done | bytes 619792
  (787 shorter events, 582.3 us)
Async XLA Ops:
  7.2 58.4 %all-gather.16.cloned.1.call-start = ((), (), s32[]{:S(2)}) async-start(), calls=%async_computation.6 | async-start | bytes 4423680 | tf_op jit(solution)/shard_map/all_gather | solution.py:229
  9.8 68.9 %all-gather.20.cloned.1.call-start = ((), (), s32[]{:S(2)}) async-start(), calls=%async_computation.8 | async-start | bytes 3317760 | tf_op jit(solution)/shard_map/all_gather | solution.py:232
  10.5 95.4 %all-gather.18.cloned.1.call-start = ((), (), s32[]{:S(2)}) async-start(), calls=%async_computation.7 | async-start | bytes 3317760 | tf_op jit(solution)/shard_map/all_gather | solution.py:231
  125.5 150.8 %all-reduce.5.cloned.1.call-start = ((), (), s32[]{:S(2)}) async-start(), calls=%async_computation.15 | async-start | bytes 6782976 | tf_op jit(solution)/shard_map/while/body/eval_jaxpr/psum | solution.py:87
  142.6 133.7 %copy-start.41 = (f32[1152]{0:T(1024)S(1)}, f32[1152]{0:T(1024)}, u32[]{:S(2)}) copy-start(f32[1152]{0:T(1024)} %get-tuple-element.1534) | copy-start | bytes 13828 | tf_op jit(solution)/shard_map/while
  145.5 276.3 %all-reduce.7.cloned.1.call-start = ((), (), s32[]{:S(2)}) async-start(), calls=%async_computation.16 | async-start | bytes 6782976 | tf_op jit(solution)/shard_map/while/body/eval_jaxpr/psum | solution.py:94
  426.0 39.8 %collective-permute-start = (bf16[1,729,1152]{2,1,0:T(8,128)(2,1)}, bf16[1,729,1152]{2,1,0:T(8,128)(2,1)}, u32[]{:S(2)}, u32[]{:S(2)}) collective-permute-start(bf16[1,729,1152]{2,1,0:T(8,128)(2,1)} %bitcast.322), channel_id=1, source_target_pairs={{0,16},{1,17},{2,18},{3,19},{4,20},{5,21},{6,22},{7,23},{8,24},{9,... | collective-permute-start | bytes 5038856 | tf_op jit(solution)/shard_map/while/body/eval_jaxpr/ppermute | solution.py:16
  465.9 150.8 %all-reduce.5.cloned.1.call-start = ((), (), s32[]{:S(2)}) async-start(), calls=%async_computation.15 | async-start | bytes 6782976 | tf_op jit(solution)/shard_map/while/body/eval_jaxpr/psum | solution.py:87
  483.0 133.7 %copy-start.41 = (f32[1152]{0:T(1024)S(1)}, f32[1152]{0:T(1024)}, u32[]{:S(2)}) copy-start(f32[1152]{0:T(1024)} %get-tuple-element.1534) | copy-start | bytes 13828 | tf_op jit(solution)/shard_map/while
  485.9 276.4 %all-reduce.7.cloned.1.call-start = ((), (), s32[]{:S(2)}) async-start(), calls=%async_computation.16 | async-start | bytes 6782976 | tf_op jit(solution)/shard_map/while/body/eval_jaxpr/psum | solution.py:94
  634.0 128.4 %copy-start.42 = (f32[1152]{0:T(1024)S(1)}, f32[1152]{0:T(1024)}, u32[]{:S(2)}) copy-start(f32[1152]{0:T(1024)} %get-tuple-element.1533) | copy-start | bytes 13828 | tf_op jit(solution)/shard_map/while
  766.5 39.8 %collective-permute-start = (bf16[1,729,1152]{2,1,0:T(8,128)(2,1)}, bf16[1,729,1152]{2,1,0:T(8,128)(2,1)}, u32[]{:S(2)}, u32[]{:S(2)}) collective-permute-start(bf16[1,729,1152]{2,1,0:T(8,128)(2,1)} %bitcast.322), channel_id=1, source_target_pairs={{0,16},{1,17},{2,18},{3,19},{4,20},{5,21},{6,22},{7,23},{8,24},{9,... | collective-permute-start | bytes 5038856 | tf_op jit(solution)/shard_map/while/body/eval_jaxpr/ppermute | solution.py:16
  806.4 150.8 %all-reduce.5.cloned.1.call-start = ((), (), s32[]{:S(2)}) async-start(), calls=%async_computation.15 | async-start | bytes 6782976 | tf_op jit(solution)/shard_map/while/body/eval_jaxpr/psum | solution.py:87
  823.4 133.7 %copy-start.41 = (f32[1152]{0:T(1024)S(1)}, f32[1152]{0:T(1024)}, u32[]{:S(2)}) copy-start(f32[1152]{0:T(1024)} %get-tuple-element.1534) | copy-start | bytes 13828 | tf_op jit(solution)/shard_map/while
  826.3 276.3 %all-reduce.7.cloned.1.call-start = ((), (), s32[]{:S(2)}) async-start(), calls=%async_computation.16 | async-start | bytes 6782976 | tf_op jit(solution)/shard_map/while/body/eval_jaxpr/psum | solution.py:94
  974.3 128.4 %copy-start.42 = (f32[1152]{0:T(1024)S(1)}, f32[1152]{0:T(1024)}, u32[]{:S(2)}) copy-start(f32[1152]{0:T(1024)} %get-tuple-element.1533) | copy-start | bytes 13828 | tf_op jit(solution)/shard_map/while
  1106.8 39.8 %collective-permute-start = (bf16[1,729,1152]{2,1,0:T(8,128)(2,1)}, bf16[1,729,1152]{2,1,0:T(8,128)(2,1)}, u32[]{:S(2)}, u32[]{:S(2)}) collective-permute-start(bf16[1,729,1152]{2,1,0:T(8,128)(2,1)} %bitcast.322), channel_id=1, source_target_pairs={{0,16},{1,17},{2,18},{3,19},{4,20},{5,21},{6,22},{7,23},{8,24},{9,... | collective-permute-start | bytes 5038856 | tf_op jit(solution)/shard_map/while/body/eval_jaxpr/ppermute | solution.py:16
  1172.1 250.1 %all-gather.22.cloned.1.call-start = ((), (), s32[]{:S(2)}) async-start(), calls=%async_computation.17 | async-start | bytes 16957440 | tf_op jit(solution)/shard_map/while/body/eval_jaxpr/all_gather | solution.py:10
  1187.7 408.0 %all-reduce.9.cloned.1.call-start = ((), (), s32[]{:S(2)}) async-start(), calls=%async_computation.18 | async-start | bytes 6782976 | tf_op jit(solution)/shard_map/while/body/eval_jaxpr/psum | solution.py:197
  1603.5 40.5 %collective-permute-start.1 = (bf16[1,729,1152]{2,1,0:T(8,128)(2,1)S(1)}, bf16[1,729,1152]{2,1,0:T(8,128)(2,1)S(1)}, u32[]{:S(2)}, u32[]{:S(2)}) collective-permute-start(bf16[1,729,1152]{2,1,0:T(8,128)(2,1)S(1)} %bitcast.386), channel_id=1, source_target_pairs={{16,0},{17,1},{18,2},{19,3},{20,4},{21,5},{22,6},{23,7},{24,8},{25... | collective-permute-start | bytes 5038856 | tf_op jit(solution)/shard_map/while/body/eval_jaxpr/ppermute | solution.py:16
  1644.3 248.2 %all-gather.22.cloned.1.call-start = ((), (), s32[]{:S(2)}) async-start(), calls=%async_computation.17 | async-start | bytes 16957440 | tf_op jit(solution)/shard_map/while/body/eval_jaxpr/all_gather | solution.py:10
  1659.9 406.1 %all-reduce.9.cloned.1.call-start = ((), (), s32[]{:S(2)}) async-start(), calls=%async_computation.18 | async-start | bytes 6782976 | tf_op jit(solution)/shard_map/while/body/eval_jaxpr/psum | solution.py:197
  2073.8 40.5 %collective-permute-start.1 = (bf16[1,729,1152]{2,1,0:T(8,128)(2,1)S(1)}, bf16[1,729,1152]{2,1,0:T(8,128)(2,1)S(1)}, u32[]{:S(2)}, u32[]{:S(2)}) collective-permute-start(bf16[1,729,1152]{2,1,0:T(8,128)(2,1)S(1)} %bitcast.386), channel_id=1, source_target_pairs={{16,0},{17,1},{18,2},{19,3},{20,4},{21,5},{22,6},{23,7},{24,8},{25... | collective-permute-start | bytes 5038856 | tf_op jit(solution)/shard_map/while/body/eval_jaxpr/ppermute | solution.py:16
  2114.5 248.2 %all-gather.22.cloned.1.call-start = ((), (), s32[]{:S(2)}) async-start(), calls=%async_computation.17 | async-start | bytes 16957440 | tf_op jit(solution)/shard_map/while/body/eval_jaxpr/all_gather | solution.py:10
  2130.2 406.1 %all-reduce.9.cloned.1.call-start = ((), (), s32[]{:S(2)}) async-start(), calls=%async_computation.18 | async-start | bytes 6782976 | tf_op jit(solution)/shard_map/while/body/eval_jaxpr/psum | solution.py:197
  2544.0 40.5 %collective-permute-start.1 = (bf16[1,729,1152]{2,1,0:T(8,128)(2,1)S(1)}, bf16[1,729,1152]{2,1,0:T(8,128)(2,1)S(1)}, u32[]{:S(2)}, u32[]{:S(2)}) collective-permute-start(bf16[1,729,1152]{2,1,0:T(8,128)(2,1)S(1)} %bitcast.386), channel_id=1, source_target_pairs={{16,0},{17,1},{18,2},{19,3},{20,4},{21,5},{22,6},{23,7},{24,8},{25... | collective-permute-start | bytes 5038856 | tf_op jit(solution)/shard_map/while/body/eval_jaxpr/ppermute | solution.py:16
  2587.6 87.4 %reduce-scatter.27.cloned.1.call-start = ((), (), s32[]{:S(2)}) async-start(), calls=%async_computation.13 | async-start | bytes 368640
  2588.6 88.0 %reduce-scatter.29.cloned.1.call-start = ((), (), s32[]{:S(2)}) async-start(), calls=%async_computation.14 | async-start | bytes 368640
  2589.6 88.6 %reduce-scatter.21.cloned.1.call-start = ((), (), s32[]{:S(2)}) async-start(), calls=%async_computation.10 | async-start | bytes 1105920
  2592.3 100.9 %reduce-scatter.19.cloned.1.call-start = ((), (), s32[]{:S(2)}) async-start(), calls=%async_computation.9 | async-start | bytes 2580480
  2606.1 124.1 %reduce-scatter.23.cloned.1.call-start = ((), (), s32[]{:S(2)}) async-start(), calls=%async_computation.11 | async-start | bytes 3317760
  2612.2 155.4 %reduce-scatter.25.cloned.1.call-start = ((), (), s32[]{:S(2)}) async-start(), calls=%async_computation.12 | async-start | bytes 3317760
  (199 other events, 1406.5 us)
Sparse Core Ops, SparseCore 0:
  10.1 40.3 all-gather.15
  52.1 26.5 all-gather.19
  80.2 25.7 all-gather.17
  145.6 130.6 all-reduce.4
  293.6 128.1 all-reduce.6
  486.0 130.6 all-reduce.4
  634.1 128.1 all-reduce.6
  826.5 130.6 all-reduce.4
  974.5 128.1 all-reduce.6
  1187.8 234.2 all-gather.21
  1469.2 126.4 all-reduce.8
  1660.0 232.3 all-gather.21
  1939.5 126.4 all-reduce.8
  2130.3 232.3 all-gather.21
  2409.7 126.4 all-reduce.8
  2591.1 18.3 reduce-scatter.26
  2612.4 20.2 reduce-scatter.28
  2635.7 23.7 reduce-scatter.20
  2662.1 30.9 reduce-scatter.18
  2695.5 34.7 reduce-scatter.22
  2732.8 34.7 reduce-scatter.24
